TPU v7x, 32 devices: a whole 2x2x4 slice. The times are simulated.
32 devices in a mesh: rep: 4 (over y, x), fsdp: 2 (over core), tp: 4 (over z).
Axes of the slice: x: 2, y: 2, z: 4, core: 2. Of those that a mesh axis runs over, the one named last changes fastest.
Arguments:
- grad_parts: bfloat16 [2, 2, 8192, 1024], P('fsdp', None, 'rep', 'tp'), may hold values from -4 to 4
- master_weight: float32 [2, 8192, 1024], P(None, ('rep', 'fsdp'), 'tp'), may hold values from -0.0625 to 0.0625
- moment_one: float32 [2, 8192, 1024], P(None, ('rep', 'fsdp'), 'tp'), may hold values from -4 to 4
- moment_two: float32 [2, 8192, 1024], P(None, ('rep', 'fsdp'), 'tp'), may hold values from 0.1 to 2
- layer_inputs: bfloat16 [384, 4, 8192], P(('rep', 'fsdp'), None, 'tp'), may hold values from -6 to 6
- queries: bfloat16 [384, 4, 8192], P(('rep', 'fsdp'), None, 'tp'), may hold values from -105 to 105
- kv_cache: bfloat16 [384, 24, 2, 1024], P(('rep', 'fsdp'), None, None, 'tp'), may hold values from -4 to 4
- lengths: int32 [384], P(('rep', 'fsdp')), may hold values from 2 to 24
Outputs:
- new_master: float32 [2, 8192, 1024], P(None, ('rep', 'fsdp'), 'tp')
- new_moment_one: float32 [2, 8192, 1024], P(None, ('rep', 'fsdp'), 'tp')
- new_moment_two: float32 [2, 8192, 1024], P(None, ('rep', 'fsdp'), 'tp')
- context: bfloat16 [384, 4, 8192], P(('rep', 'fsdp'), None, 'tp')
Inputs may be any that keep to these rules, and one draw needn't show every extreme that they name: lengths[r] is the number of valid cached positions of row r, at most 24.
All inputs are finite; a program needn't handle non-finite values.
Results may differ from a plain program's by a relative error of at most 0.0065.
Values may be sent and summed in bfloat16 or wider, within the bound.
A program may use at most 64 MiB of HBM per device.

v0:
```python
import jax
import jax.numpy as jnp
from jax import lax
from jax.sharding import PartitionSpec as P

HD = 128
beta_one = 0.9
beta_two = 0.95
learning_rate = 0.001
weight_decay = 0.1
epsilon = 1e-08
first_bias = 1.0 - 0.9**10
second_bias = 1.0 - 0.95**10


def adamw_update(gradient, master, moment_one, moment_two):
    new_one = beta_one * moment_one + (1.0 - beta_one) * gradient
    new_two = beta_two * moment_two + (1.0 - beta_two) * gradient * gradient
    update = new_one / first_bias / (jnp.sqrt(new_two / second_bias) + epsilon)
    new_master = master - learning_rate * (update + weight_decay * master)
    return (new_one, new_two, new_master)


def attend(queries, kv_cache, fresh_keys, fresh_values, lengths):
    row_count = queries.shape[0]
    step_count = queries.shape[1]
    kv_heads = fresh_keys.shape[2]
    cache_len = kv_cache.shape[1]
    grouped = queries.reshape(row_count, step_count, kv_heads, -1, HD)
    cached_keys = kv_cache[:, :, 0].reshape(row_count, cache_len, kv_heads, HD)
    cached_values = kv_cache[:, :, 1].reshape(row_count, cache_len, kv_heads, HD)
    scaling = 1.0 / jnp.sqrt(jnp.float32(HD))
    cached_scores = (
        jnp.einsum("rsgqd,rcgd->rsgqc", grouped, cached_keys, preferred_element_type=jnp.float32)
        * scaling
    )
    fresh_scores = (
        jnp.einsum("rsgqd,rugd->rsgqu", grouped, fresh_keys, preferred_element_type=jnp.float32)
        * scaling
    )
    valid_old = jnp.arange(cache_len, dtype=jnp.int32)[None, :] < lengths[:, None]
    valid_old = valid_old[:, None, None, None, :]
    steps_index = jnp.arange(step_count, dtype=jnp.int32)
    valid_new = (steps_index[None, :] <= steps_index[:, None])[None, :, None, None, :]
    scores = jnp.concatenate(
        [
            jnp.where(valid_old, cached_scores, -jnp.inf),
            jnp.where(valid_new, fresh_scores, -jnp.inf),
        ],
        axis=-1,
    )
    row_max = jnp.max(scores, axis=-1, keepdims=True)
    exponent = jnp.exp(scores - row_max)
    weights = (exponent / jnp.sum(exponent, axis=-1, keepdims=True)).astype(jnp.bfloat16)
    output = jnp.einsum(
        "rsgqc,rcgd->rsgqd",
        weights[..., :cache_len],
        cached_values,
        preferred_element_type=jnp.float32,
    )
    output = output + jnp.einsum(
        "rsgqu,rugd->rsgqd",
        weights[..., cache_len:],
        fresh_values,
        preferred_element_type=jnp.float32,
    )
    return output.astype(jnp.bfloat16).reshape(row_count, step_count, -1)


def on_device(
    grad_parts, master_weight, moment_one, moment_two, layer_inputs, queries, kv_cache, lengths
):
    gradient = lax.psum_scatter(
        grad_parts[0].astype(jnp.float32).astype(jnp.bfloat16),
        "fsdp",
        scatter_dimension=1,
        tiled=True,
    ).astype(jnp.float32)
    new_one, new_two, new_master = adamw_update(gradient, master_weight, moment_one, moment_two)
    rollout_weight = new_master.astype(jnp.bfloat16)
    row_count = layer_inputs.shape[0]
    step_count = layer_inputs.shape[1]
    gathered = lax.all_gather(layer_inputs, "tp", axis=2, tiled=True)
    flattened = gathered.reshape(row_count * step_count, gathered.shape[2])
    projected = jnp.einsum(
        "td,kdc->ktc",
        flattened,
        lax.all_gather(rollout_weight, ("rep", "fsdp"), axis=1, tiled=True),
        preferred_element_type=jnp.float32,
    )
    fresh_pair = projected.astype(jnp.bfloat16).reshape(2, row_count, step_count, -1, HD)
    context = attend(queries, kv_cache, fresh_pair[0], fresh_pair[1], lengths)
    return (new_master, new_one, new_two, context)


def solution(mesh):
    return jax.shard_map(
        on_device,
        mesh=mesh,
        in_specs=(
            P("fsdp", None, "rep", "tp"),
            P(None, ("rep", "fsdp"), "tp"),
            P(None, ("rep", "fsdp"), "tp"),
            P(None, ("rep", "fsdp"), "tp"),
            P(("rep", "fsdp"), None, "tp"),
            P(("rep", "fsdp"), None, "tp"),
            P(("rep", "fsdp"), None, None, "tp"),
            P(("rep", "fsdp")),
        ),
        out_specs=(
            P(None, ("rep", "fsdp"), "tp"),
            P(None, ("rep", "fsdp"), "tp"),
            P(None, ("rep", "fsdp"), "tp"),
            P(("rep", "fsdp"), None, "tp"),
        ),
        check_vma=False,
    )
```

profile of v0, /device:TPU:0, one launch (start us, length us, event | category | flops | bytes accessed | tf_op | source)
XLA Modules:
  0.0 160.2 jit_solution(18076196282730567113)
XLA Ops:
  8.0 0.0 reduce-scatter.2.cloned.1.call-start
  8.1 0.7 reduce-scatter.2.cloned.1.call-update
  8.7 0.0 all-gather.5.cloned.1.call-start
  8.8 0.5 all-gather.5.cloned.1.call-update
  9.3 0.0 all-gather.3.cloned.1.call-start
  9.4 14.2 %reduce-scatter.2.cloned.1.call-done = bf16[2,1024,256]{2,1,0:T(8,128)(2,1)} async-done(((bf16[2,2048,256]{2,1,0:T(8,128)(2,1)}), bf16[2,1024,256]{2,1,0:T(8,128)(2,1)}) %reduce-scatter.2.cloned.1.call-update) | async-done | bytes 1048592 | tf_op jit(solution)/shard_map/reduce_scatter | solution.py:73
  23.6 6.7 %fusion.17 = (bf16[2,1024,256]{2,1,0:T(8,128)(2,1)}, f32[2,1024,256]{2,1,0:T(8,128)}, f32[2,1024,256]{2,1,0:T(8,128)}, f32[2,1024,256]{2,1,0:T(8,128)}) fusion(f32[2,1024,256]{2,1,0:T(8,128)S(1)} %copy-done.2, bf16[2,1024,256]{2,1,0:T(8,128)(2,1)} %reduce-scatter.2.cloned.1.call-done, f32[2,1024,256]{2,1,0:T(8,128)} %param.10, f32[2,1024,256]{2,1,0:T(8,128)} %param.11), kind=kLoop, calls=%fused_computation.30 | loop fusion | flops 8912896 | bytes 14680064 | tf_op jit(solution)/shard_map/convert_element_type | solution.py:80
  30.2 0.0 all-gather.3.cloned.1.call-update
  30.3 0.5 reshape.57
  30.8 0.7 copy-done.1
  31.5 4.9 %slice_reduce_fusion = (bf16[48,24,256]{2,1,0:T(8,128)(2,1)S(1)}, bf16[48,24,256]{2,1,0:T(8,128)(2,1)S(1)}) fusion(bf16[48,24,2,256]{3,2,1,0:T(2,128)(2,1)S(1)} %copy-done.1), kind=kLoop, calls=%fused_computation.11 | loop fusion | bytes 2359296 | tf_op jit(solution)/shard_map/slice | solution.py:31
  36.4 1.0 reshape_squeeze.6
  37.4 1.0 reshape_squeeze.7
  38.3 0.1 iota_compare_fusion
  38.4 1.7 %fusion.21 = (f32[48,4,2,8]{3,1,2,0:T(4,128)S(1)}, f32[48,4,2,8,24]{4,3,1,2,0:T(8,128)S(1)}) fusion(bf16[48,4,2,8,128]{4,3,2,1,0:T(8,128)(2,1)S(1)} %reshape.57, bf16[48,24,2,128,1]{3,2,1,0,4:T(2,128)(2,1)} %bitcast.23, pred[48,24]{1,0:T(8,128)(4,1)S(1)} %iota_compare_fusion), kind=kOutput, calls=%fused_computation.32 | convolution fusion | flops 19092480 | bytes 1684608 | tf_op jit(solution)/shard_map/rsgqd,rcgd->rsgqc/dot_general | solution.py:34
  40.1 36.7 %all-gather.5.cloned.1.call-done = bf16[48,4,8192]{2,1,0:T(4,128)(2,1)} async-done(((bf16[48,4,2048]{2,1,0:T(4,128)(2,1)}), bf16[48,4,8192]{2,1,0:T(4,128)(2,1)}) %all-gather.5.cloned.1.call-update) | async-done | bytes 3145744 | tf_op jit(solution)/shard_map/all_gather | solution.py:83
  76.9 5.5 %reshape.61 = bf16[192,8192,1]{1,0,2:T(8,128)(2,1)} reshape(bf16[48,4,8192]{2,1,0:T(4,128)(2,1)} %all-gather.5.cloned.1.call-done) | data formatting | bytes 6291456 | tf_op jit(solution)/shard_map/reshape | solution.py:84
  82.3 49.1 %all-gather.3.cloned.1.call-done = bf16[2,8192,256]{2,1,0:T(8,128)(2,1)} async-done(((bf16[2,1024,256]{2,1,0:T(8,128)(2,1)}), bf16[2,8192,256]{2,1,0:T(8,128)(2,1)}) %all-gather.3.cloned.1.call-update) | async-done | bytes 8388624 | tf_op jit(solution)/shard_map/all_gather | solution.py:88
  131.4 6.1 %fusion.4 = bf16[2,192,256]{2,1,0:T(8,128)(2,1)S(1)} fusion(bf16[192,8192,1]{1,0,2:T(8,128)(2,1)} %reshape.61, bf16[2,8192,256]{2,1,0:T(8,128)(2,1)} %all-gather.3.cloned.1.call-done), kind=kOutput, calls=%fused_computation.14 | convolution fusion | flops 1610711040 | bytes 11730944 | tf_op jit(solution)/shard_map/td,kdc->ktc/dot_general | solution.py:85
  137.6 0.6 fusion.20
  138.2 3.5 %fusion.8 = f32[48,2,4,4,8]{4,2,3,1,0:T(4,128)S(1)} fusion(bf16[48,4,2,8,128]{4,3,2,1,0:T(8,128)(2,1)S(1)} %reshape.57, bf16[48,4,2,128,1]{3,2,1,0,4:T(2,128)(2,1)S(1)} %bitcast.26), kind=kOutput, calls=%fused_computation.18 | convolution fusion | flops 3145728 | bytes 933888 | tf_op jit(solution)/shard_map/rsgqd,rugd->rsgqu/dot_general | solution.py:38
  141.8 0.5 copy.55
  142.3 0.7 fusion.16
  143.0 0.1 copy.57
  143.2 2.4 %copy.56 = f32[48,4,2,8,4]{4,3,1,2,0:T(8,128)S(1)} copy(f32[48,4,2,8,4]{0,3,1,4,2:T(8,128)} %get-tuple-element.23) | data formatting | bytes 98304 | tf_op jit(solution)/shard_map/jit(_where)/select_n | solution.py:48
  145.5 0.1 reduce_max.22
  145.6 1.5 fusion.13
  147.1 2.2 %divide_convert_fusion = bf16[48,4,2,8,28]{4,3,1,2,0:T(8,128)(2,1)} fusion(f32[48,4,2,8]{3,1,2,0:T(4,128)S(1)} %fusion.13, f32[48,4,2,8]{3,1,2,0:T(4,128)S(1)} %reduce_max.22, f32[48,4,2,8,4]{4,3,1,2,0:T(8,128)S(1)} %copy.56, f32[48,4,2,8,24]{4,3,1,2,0:T(8,128)S(1)} %get-tuple-element.31), kind=kLoop, calls=%fused_computation.9 | loop fusion | flops 344064 | bytes 540672 | tf_op jit(solution)/shard_map/convert_element_type | solution.py:54
  149.3 1.7 %fusion.6 = f32[48,2,4,8,128]{4,3,2,1,0:T(8,128)S(1)} fusion(bf16[48,4,2,8,28]{4,3,1,2,0:T(8,128)(2,1)} %divide_convert_fusion, bf16[48,24,2,128,1]{3,2,1,0,4:T(2,128)(2,1)} %bitcast.22), kind=kOutput, calls=%fused_computation.16 | convolution fusion | flops 18874368 | bytes 2334720 | tf_op jit(solution)/shard_map/rsgqc,rcgd->rsgqd/dot_general | solution.py:55
  151.1 0.4 fusion.3
  151.5 0.1 copy.76
  151.7 1.1 reshape.66
  (14 shorter events, 0.1 us)
Async XLA Ops:
  8.0 15.6 %copy-start.2 = (f32[2,1024,256]{2,1,0:T(8,128)S(1)}, f32[2,1024,256]{2,1,0:T(8,128)}, u32[]{:S(2)}) copy-start(f32[2,1024,256]{2,1,0:T(8,128)} %param.9) | copy-start | bytes 6291460
  8.0 15.6 %reduce-scatter.2.cloned.1.call-start = ((), (), s32[]{:S(2)}) async-start(), calls=%async_computation.1 | async-start | bytes 3145728 | tf_op jit(solution)/shard_map/reduce_scatter | solution.py:73
  8.7 68.1 %all-gather.5.cloned.1.call-start = ((), (), s32[]{:S(2)}) async-start(), calls=%async_computation.3 | async-start | bytes 3932160 | tf_op jit(solution)/shard_map/all_gather | solution.py:83
  9.3 20.9 %copy-start.3 = (bf16[48,4,2048]{2,1,0:T(4,128)(2,1)S(1)}, bf16[48,4,2048]{2,1,0:T(4,128)(2,1)}, u32[]{:S(2)}) copy-start(bf16[48,4,2048]{2,1,0:T(4,128)(2,1)} %param.13) | copy-start | bytes 2359300
  9.3 122.1 %all-gather.3.cloned.1.call-start = ((), (), s32[]{:S(2)}) async-start(), calls=%async_computation.2 | async-start | bytes 9437184 | tf_op jit(solution)/shard_map/all_gather | solution.py:88
  30.2 1.3 copy-start.1
  31.5 6.8 %copy-start.5 = (s32[48]{0:T(128)S(1)}, s32[48]{0:T(128)}, u32[]{:S(2)}) copy-start(s32[48]{0:T(128)} %param.15) | copy-start | bytes 580
  147.1 2.2 %copy-start.4 = (bf16[1,192,256]{2,1,0:T(8,128)(2,1)S(1)}, bf16[1,192,256]{2,1,0:T(8,128)(2,1)}, u32[]{:S(2)}) copy-start(bf16[1,192,256]{2,1,0:T(8,128)(2,1)} %get-tuple-element.28) | copy-start | bytes 294916
  149.3 1.8 %copy-start = (bf16[48,4,2,8,28]{4,3,1,2,0:T(8,128)(2,1)S(1)}, bf16[48,4,2,8,28]{4,3,1,2,0:T(8,128)(2,1)}, u32[]{:S(2)}) copy-start(bf16[48,4,2,8,28]{4,3,1,2,0:T(8,128)(2,1)} %divide_convert_fusion) | copy-start | bytes 516100
Sparse Core Ops, SparseCore 0:
  11.1 12.4 reduce-scatter.1
Sparse Core Ops, SparseCore 1:
  10.8 66.0 all-gather.4
  78.6 52.8 all-gather.2
where the time goes:
time: 161 us; the launch traced here: 160 us
  waiting for transfers between devices  101 us (63%)
  local copies, waits for them, and re-layouts  18.4 us (11%)
  between operations  15.6 us (10%)
  matrix products  13.6 us (8%)
  other arithmetic  11.2 us (7%)
    all_gather x1, waiting for transfers between devices, on_device(): lax.all_gather(rollout_weight, ('rep', 'fsdp'), axis=1, tiled=True)  49.1 us
    all_gather x1, waiting for transfers between devices, on_device(): gathered = lax.all_gather(layer_inputs, 'tp', axis=2, tiled=True)  36.7 us
    reduce_scatter x1, waiting for transfers between devices, on_device(): lax.psum_scatter(grad_parts[0].astype(jnp.float32).astype(jnp.bfloat16),...  14.2 us
    convert_element_type x1, other arithmetic, on_device(): rollout_weight = new_master.astype(jnp.bfloat16)  6.66 us
    dot_general x1, matrix products, on_device(): jnp.einsum('td,kdc->ktc', flattened, lax.all_gather(rollout_weight, ('rep...  6.13 us
    reshape x1, local copies, waits for them, and re-layouts, on_device(): flattened = gathered.reshape(row_count * step_count, gathered.shape[2])  5.49 us
    slice x1, local copies, waits for them, and re-layouts, attend(): kv_cache[:, :, 1].reshape(row_count, cache_len, kv_heads, HD)  4.9 us
    dot_general x1, matrix products, attend(): jnp.einsum('rsgqd,rugd->rsgqu', grouped, fresh_keys, preferred_element_ty...  3.54 us
  transfers between devices with their start and end apart: 3, of which 3 were waited for; matrix products, arithmetic and copies ran while one was open for 13% of the time, Pallas kernels for 0%

commit v1 on v0

--- a/solution.py
+++ b/solution.py
@@ -80,7 +80,12 @@
     rollout_weight = new_master.astype(jnp.bfloat16)
     row_count = layer_inputs.shape[0]
     step_count = layer_inputs.shape[1]
-    gathered = lax.all_gather(layer_inputs, "tp", axis=2, tiled=True)
+    ring = [layer_inputs]
+    for hop in range(3):
+        ring.append(lax.ppermute(ring[-1], "tp", [(dev, (dev + 1) % 4) for dev in range(4)]))
+    gathered = jnp.roll(
+        jnp.concatenate(ring[::-1], axis=2), (lax.axis_index("tp") + 1) * ring[0].shape[2], axis=2
+    )
     flattened = gathered.reshape(row_count * step_count, gathered.shape[2])
     projected = jnp.einsum(
         "td,kdc->ktc",

time: 161 us -> 139 us (0.86)
  waiting for transfers between devices: 101 us -> 63.1 us
  local copies, waits for them, and re-layouts: 18.4 us -> 33.3 us
  starting transfers between devices: 0.12 us -> 1.98 us
    all_gather x1, waiting for transfers between devices: 49.1 us -> 0.01 us  [on_device(): lax.all_gather(rollout_weight, ('rep', 'fsdp'), axis=1, tiled=True)]
    ppermute x0 -> x3, waiting for transfers between devices: none -> 47.6 us  [on_device(): lax.ppermute(ring[-1], 'tp', [(dev, (dev + 1) % 4) for dev in range(4)])]
    all_gather x1 -> x0, waiting for transfers between devices: 36.7 us -> none  [on_device(): gathered = lax.all_gather(layer_inputs, 'tp', axis=2, tiled=True)]
    unnamed x14 -> x25, local copies, waits for them, and re-layouts: 1.95 us -> 8.69 us
    dynamic_slice x0 -> x1, local copies, waits for them, and re-layouts: none -> 3.07 us  [on_device(): jnp.roll(jnp.concatenate(ring[::-1], axis=2), (lax.axis_index('tp') + 1)...]
    ppermute x0 -> x3, starting transfers between devices: none -> 1.91 us  [on_device(): lax.ppermute(ring[-1], 'tp', [(dev, (dev + 1) % 4) for dev in range(4)])]
  transfers between devices with their start and end apart: 3 -> 5, of which waited for: 3 -> 4; matrix products, arithmetic and copies ran while one was open for 13% -> 21% of each run, Pallas kernels for 0% -> 0%
where the time goes in v1:
time: 139 us
  waiting for transfers between devices  63.1 us (45%)
  local copies, waits for them, and re-layouts  33.3 us (24%)
  between operations  14.2 us (10%)
  matrix products  13.6 us (10%)
  other arithmetic  12.6 us (9%)
  starting transfers between devices  1.98 us (1%)
    ppermute x3, waiting for transfers between devices, on_device(): lax.ppermute(ring[-1], 'tp', [(dev, (dev + 1) % 4) for dev in range(4)])  47.6 us
    reduce_scatter x1, waiting for transfers between devices, on_device(): lax.psum_scatter(grad_parts[0].astype(jnp.float32).astype(jnp.bfloat16),...  14.8 us
    unnamed x25, local copies, waits for them, and re-layouts  8.69 us
    convert_element_type x1, other arithmetic, on_device(): rollout_weight = new_master.astype(jnp.bfloat16)  7.37 us
    dot_general x1, matrix products, on_device(): jnp.einsum('td,kdc->ktc', flattened, lax.all_gather(rollout_weight, ('rep...  6.13 us
    slice x1, local copies, waits for them, and re-layouts, attend(): kv_cache[:, :, 1].reshape(row_count, cache_len, kv_heads, HD)  5.88 us
    reshape x1, local copies, waits for them, and re-layouts, on_device(): flattened = gathered.reshape(row_count * step_count, gathered.shape[2])  5.48 us
    dot_general x1, matrix products, attend(): jnp.einsum('rsgqd,rugd->rsgqu', grouped, fresh_keys, preferred_element_ty...  3.54 us
  transfers between devices with their start and end apart: 5, of which 4 were waited for; matrix products, arithmetic and copies ran while one was open for 21% of the time, Pallas kernels for 0%

profile of v1, /device:TPU:0, one launch (start us, length us, event | category | flops | bytes accessed | tf_op | source)
XLA Modules:
  0.0 138.8 jit_solution(11561586046683696303)
XLA Ops:
  7.2 0.7 reduce-scatter.2.cloned.1.call-update
  8.0 14.8 %reduce-scatter.2.cloned.1.call-done = bf16[2,1024,256]{2,1,0:T(8,128)(2,1)} async-done(((bf16[2,2048,256]{2,1,0:T(8,128)(2,1)}), bf16[2,1024,256]{2,1,0:T(8,128)(2,1)}) %reduce-scatter.2.cloned.1.call-update) | async-done | bytes 1048592 | tf_op jit(solution)/shard_map/reduce_scatter | solution.py:73
  22.7 7.4 %fusion.17 = (bf16[2,1024,256]{2,1,0:T(8,128)(2,1)}, f32[2,1024,256]{2,1,0:T(8,128)}, f32[2,1024,256]{2,1,0:T(8,128)}, f32[2,1024,256]{2,1,0:T(8,128)}) fusion(f32[2,1024,256]{2,1,0:T(8,128)} %param.9, bf16[2,1024,256]{2,1,0:T(8,128)(2,1)} %reduce-scatter.2.cloned.1.call-done, f32[2,1024,256]{2,1,0:T(8,128)} %param.10, f32[2,1024,256]{2,1,0:T(8,128)} %param.11), kind=kLoop, calls=%fused_computation.39 | loop fusion | flops 8912896 | bytes 14680064 | tf_op jit(solution)/shard_map/convert_element_type | solution.py:80
  30.1 1.9 %collective-permute-start = (bf16[48,4,2048]{2,1,0:T(4,128)(2,1)S(1)}, bf16[48,4,2048]{2,1,0:T(4,128)(2,1)S(1)}, u32[]{:S(2)}, u32[]{:S(2)}) collective-permute-start(bf16[48,4,2048]{2,1,0:T(4,128)(2,1)S(1)} %copy-done.2), channel_id=1, source_target_pairs={{0,1},{1,2},{2,3},{3,0},{4,5},{5,6},{6,7},{7,4},{8,9},{9,10},{10,1... | collective-permute-start | bytes 2359304 | tf_op jit(solution)/shard_map/ppermute | solution.py:85
  32.0 19.7 %collective-permute-done = bf16[48,4,2048]{2,1,0:T(4,128)(2,1)S(1)} collective-permute-done((bf16[48,4,2048]{2,1,0:T(4,128)(2,1)S(1)}, bf16[48,4,2048]{2,1,0:T(4,128)(2,1)S(1)}, u32[]{:S(2)}, u32[]{:S(2)}) %collective-permute-start) | collective-permute-done | bytes 786464 | tf_op jit(solution)/shard_map/ppermute | solution.py:85
  51.8 20.8 %collective-permute-done.1 = bf16[48,4,2048]{2,1,0:T(4,128)(2,1)} collective-permute-done((bf16[48,4,2048]{2,1,0:T(4,128)(2,1)S(1)}, bf16[48,4,2048]{2,1,0:T(4,128)(2,1)}, u32[]{:S(2)}, u32[]{:S(2)}) %collective-permute-start.1) | collective-permute-done | bytes 786464 | tf_op jit(solution)/shard_map/ppermute | solution.py:85
  72.6 5.9 %slice_reduce_fusion = (bf16[48,24,256]{2,1,0:T(8,128)(2,1)}, bf16[48,24,256]{2,1,0:T(8,128)(2,1)}) fusion(bf16[48,24,2,256]{3,2,1,0:T(2,128)(2,1)S(1)} %copy-done.1), kind=kLoop, calls=%fused_computation.11 | loop fusion | bytes 2359296 | tf_op jit(solution)/shard_map/slice | solution.py:31
  78.5 1.9 %reshape.57 = bf16[48,4,2,8,128]{4,3,2,1,0:T(8,128)(2,1)S(1)} reshape(bf16[48,4,2048]{2,1,0:T(4,128)(2,1)} %param.13) | data formatting | bytes 1572864 | tf_op jit(solution)/shard_map/reshape | solution.py:29
  80.4 2.5 %reshape_squeeze.6 = bf16[48,24,2,128]{3,2,1,0:T(2,128)(2,1)} reshape(bf16[48,24,256]{2,1,0:T(8,128)(2,1)} %get-tuple-element.21) | data formatting | bytes 1179648 | tf_op jit(solution)/shard_map/reshape;squeeze | solution.py:30
  82.8 0.9 reshape_squeeze.7
  83.9 1.7 %fusion.21 = (f32[48,4,2,8]{3,1,2,0:T(4,128)S(1)}, f32[48,4,2,8,24]{4,3,1,2,0:T(8,128)S(1)}) fusion(bf16[48,4,2,8,128]{4,3,2,1,0:T(8,128)(2,1)S(1)} %reshape.57, bf16[48,24,2,128,1]{3,2,1,0,4:T(2,128)(2,1)} %bitcast.23, pred[48,24]{1,0:T(8,128)(4,1)S(1)} %iota_compare_fusion), kind=kOutput, calls=%fused_computation.41 | convolution fusion | flops 19092480 | bytes 1684608 | tf_op jit(solution)/shard_map/rsgqd,rcgd->rsgqc/dot_general | solution.py:34
  85.6 7.1 %collective-permute-done.2 = bf16[48,4,2048]{2,1,0:T(4,128)(2,1)} collective-permute-done((bf16[48,4,2048]{2,1,0:T(4,128)(2,1)}, bf16[48,4,2048]{2,1,0:T(4,128)(2,1)}, u32[]{:S(2)}, u32[]{:S(2)}) %collective-permute-start.2) | collective-permute-done | bytes 786464 | tf_op jit(solution)/shard_map/ppermute | solution.py:85
  92.7 1.5 %constant_dynamic-update-slice_fusion.7 = bf16[48,4,16384]{2,1,0:T(4,128)(2,1)S(1)} fusion(bf16[48,4,2048]{2,1,0:T(4,128)(2,1)} %collective-permute-done.2), kind=kLoop, calls=%fused_computation.35 | loop fusion | bytes 1572864
  94.2 1.6 %constant_dynamic-update-slice_fusion.6 = bf16[48,4,16384]{2,1,0:T(4,128)(2,1)S(1)} fusion(bf16[48,4,16384]{2,1,0:T(4,128)(2,1)S(1)} %constant_dynamic-update-slice_fusion.7, bf16[48,4,2048]{2,1,0:T(4,128)(2,1)} %collective-permute-done.1), kind=kLoop, calls=%fused_computation.34 | loop fusion | bytes 1572864
  95.8 0.4 constant_dynamic-update-slice_fusion.5
  96.7 1.6 %constant_dynamic-update-slice_fusion.3 = bf16[48,4,16384]{2,1,0:T(4,128)(2,1)S(1)} fusion(bf16[48,4,16384]{2,1,0:T(4,128)(2,1)S(1)} %constant_dynamic-update-slice_fusion.4, bf16[48,4,2048]{2,1,0:T(4,128)(2,1)} %collective-permute-done.2), kind=kLoop, calls=%fused_computation.31 | loop fusion | bytes 1572864
  98.3 1.6 %constant_dynamic-update-slice_fusion.2 = bf16[48,4,16384]{2,1,0:T(4,128)(2,1)S(1)} fusion(bf16[48,4,16384]{2,1,0:T(4,128)(2,1)S(1)} %constant_dynamic-update-slice_fusion.3, bf16[48,4,2048]{2,1,0:T(4,128)(2,1)} %collective-permute-done.1), kind=kLoop, calls=%fused_computation.30 | loop fusion | bytes 1572864
  99.8 0.4 constant_dynamic-update-slice_fusion.1
  100.7 3.1 %constant_dynamic-slice_fusion = bf16[48,4,8192]{2,1,0:T(4,128)(2,1)} fusion(bf16[48,4,16384]{2,1,0:T(4,128)(2,1)S(1)} %constant_dynamic-update-slice_fusion, s32[]{:T(128)S(6)} %select_n.27), kind=kLoop, calls=%fused_computation.37 | loop fusion | bytes 6291460 | tf_op jit(solution)/shard_map/jit(_roll_dynamic)/dynamic_slice | solution.py:86
  103.8 5.5 %reshape.61 = bf16[192,8192,1]{1,0,2:T(8,128)(2,1)} reshape(bf16[48,4,8192]{2,1,0:T(4,128)(2,1)} %constant_dynamic-slice_fusion) | data formatting | bytes 6291456 | tf_op jit(solution)/shard_map/reshape | solution.py:89
  109.3 6.1 %fusion.4 = bf16[2,192,256]{2,1,0:T(8,128)(2,1)S(1)} fusion(bf16[192,8192,1]{1,0,2:T(8,128)(2,1)} %reshape.61, bf16[2,8192,256]{2,1,0:T(8,128)(2,1)} %all-gather.2.cloned.1.call-done), kind=kOutput, calls=%fused_computation.14 | convolution fusion | flops 1610711040 | bytes 11730944 | tf_op jit(solution)/shard_map/td,kdc->ktc/dot_general | solution.py:90
  115.4 0.7 fusion.20
  116.1 3.5 %fusion.8 = f32[48,2,4,4,8]{4,2,3,1,0:T(4,128)S(1)} fusion(bf16[48,4,2,8,128]{4,3,2,1,0:T(8,128)(2,1)S(1)} %reshape.57, bf16[48,4,2,128,1]{3,2,1,0,4:T(2,128)(2,1)S(1)} %bitcast.26), kind=kOutput, calls=%fused_computation.18 | convolution fusion | flops 3145728 | bytes 933888 | tf_op jit(solution)/shard_map/rsgqd,rugd->rsgqu/dot_general | solution.py:38
  119.6 0.5 copy.55
  120.1 1.4 fusion.16
  121.5 2.4 %copy.56 = f32[48,4,2,8,4]{4,3,1,2,0:T(8,128)S(1)} copy(f32[48,4,2,8,4]{0,3,1,4,2:T(8,128)} %get-tuple-element.23) | data formatting | bytes 98304 | tf_op jit(solution)/shard_map/jit(_where)/select_n | solution.py:48
  123.8 0.9 copy.57
  124.8 1.5 %fusion.13 = f32[48,4,2,8]{3,1,2,0:T(4,128)S(1)} fusion(f32[48,4,2,8]{3,1,2,0:T(4,128)S(1)} %reduce_max.22, f32[48,4,2,8,4]{4,3,1,2,0:T(8,128)S(1)} %copy.56, f32[48,4,2,8,24]{4,3,1,2,0:T(8,128)S(1)} %get-tuple-element.31), kind=kLoop, calls=%fused_computation.23 | loop fusion | flops 254976 | bytes 368640 | tf_op jit(solution)/shard_map/reduce_sum | solution.py:54
  126.3 2.2 %divide_convert_fusion = bf16[48,4,2,8,28]{4,3,1,2,0:T(8,128)(2,1)} fusion(f32[48,4,2,8]{3,1,2,0:T(4,128)S(1)} %fusion.13, f32[48,4,2,8]{3,1,2,0:T(4,128)S(1)} %reduce_max.22, f32[48,4,2,8,4]{4,3,1,2,0:T(8,128)S(1)} %copy.56, f32[48,4,2,8,24]{4,3,1,2,0:T(8,128)S(1)} %get-tuple-element.31), kind=kLoop, calls=%fused_computation.9 | loop fusion | flops 344064 | bytes 540672 | tf_op jit(solution)/shard_map/convert_element_type | solution.py:54
  128.5 1.7 %fusion.6 = f32[48,2,4,8,128]{4,3,2,1,0:T(8,128)S(1)} fusion(bf16[48,4,2,8,28]{4,3,1,2,0:T(8,128)(2,1)} %divide_convert_fusion, bf16[48,24,2,128,1]{3,2,1,0,4:T(2,128)(2,1)} %bitcast.22), kind=kOutput, calls=%fused_computation.16 | convolution fusion | flops 18874368 | bytes 2334720 | tf_op jit(solution)/shard_map/rsgqc,rcgd->rsgqd/dot_general | solution.py:55
  130.3 0.4 fusion.3
  130.9 1.1 reshape.66
  (30 shorter events, 1.3 us)
Async XLA Ops:
  7.2 15.6 %reduce-scatter.2.cloned.1.call-start = ((), (), s32[]{:S(2)}) async-start(), calls=%async_computation.1 | async-start | bytes 3145728 | tf_op jit(solution)/shard_map/reduce_scatter | solution.py:73
  7.9 22.2 %copy-start.2 = (bf16[48,4,2048]{2,1,0:T(4,128)(2,1)S(1)}, bf16[48,4,2048]{2,1,0:T(4,128)(2,1)}, u32[]{:S(2)}) copy-start(bf16[48,4,2048]{2,1,0:T(4,128)(2,1)} %param.12) | copy-start | bytes 2359300
  7.9 101.3 %all-gather.2.cloned.1.call-start = ((), (), s32[]{:S(2)}) async-start(), calls=%async_computation.2 | async-start | bytes 9437184 | tf_op jit(solution)/shard_map/all_gather | solution.py:93
  22.7 49.9 %copy-start.1 = (bf16[48,24,2,256]{3,2,1,0:T(2,128)(2,1)S(1)}, bf16[48,24,2,256]{3,2,1,0:T(2,128)(2,1)}, u32[]{:S(2)}) copy-start(bf16[48,24,2,256]{3,2,1,0:T(2,128)(2,1)} %param.14) | copy-start | bytes 3538948
  30.1 21.6 %collective-permute-start = (bf16[48,4,2048]{2,1,0:T(4,128)(2,1)S(1)}, bf16[48,4,2048]{2,1,0:T(4,128)(2,1)S(1)}, u32[]{:S(2)}, u32[]{:S(2)}) collective-permute-start(bf16[48,4,2048]{2,1,0:T(4,128)(2,1)S(1)} %copy-done.2), channel_id=1, source_target_pairs={{0,1},{1,2},{2,3},{3,0},{4,5},{5,6},{6,7},{7,4},{8,9},{9,10},{10,1... | collective-permute-start | bytes 2359304 | tf_op jit(solution)/shard_map/ppermute | solution.py:85
  51.8 26.7 %copy-start.3 = (bf16[48,4,2048]{2,1,0:T(4,128)(2,1)}, bf16[48,4,2048]{2,1,0:T(4,128)(2,1)S(1)}, u32[]{:S(2)}) copy-start(bf16[48,4,2048]{2,1,0:T(4,128)(2,1)S(1)} %collective-permute-done) | copy-start | bytes 2359300
  51.8 20.8 %collective-permute-start.1 = (bf16[48,4,2048]{2,1,0:T(4,128)(2,1)S(1)}, bf16[48,4,2048]{2,1,0:T(4,128)(2,1)}, u32[]{:S(2)}, u32[]{:S(2)}) collective-permute-start(bf16[48,4,2048]{2,1,0:T(4,128)(2,1)S(1)} %collective-permute-done), channel_id=1, source_target_pairs={{0,1},{1,2},{2,3},{3,0},{4,5},{5,6},{6,7},{7,4},{8,9},{9,10},{10,1... | collective-permute-start | bytes 2359304 | tf_op jit(solution)/shard_map/ppermute | solution.py:85
  72.6 20.2 %collective-permute-start.2 = (bf16[48,4,2048]{2,1,0:T(4,128)(2,1)}, bf16[48,4,2048]{2,1,0:T(4,128)(2,1)}, u32[]{:S(2)}, u32[]{:S(2)}) collective-permute-start(bf16[48,4,2048]{2,1,0:T(4,128)(2,1)} %collective-permute-done.1), channel_id=1, source_target_pairs={{0,1},{1,2},{2,3},{3,0},{4,5},{5,6},{6,7},{7,4},{8,9},{9,10},{10,1... | collective-permute-start | bytes 2359304 | tf_op jit(solution)/shard_map/ppermute | solution.py:85
  78.5 4.4 %copy-start.5 = (bf16[48,24,256]{2,1,0:T(8,128)(2,1)S(1)}, bf16[48,24,256]{2,1,0:T(8,128)(2,1)}, u32[]{:S(2)}) copy-start(bf16[48,24,256]{2,1,0:T(8,128)(2,1)} %get-tuple-element.20) | copy-start | bytes 1769476
  78.5 5.3 %copy-start.7 = (s32[48]{0:T(128)S(1)}, s32[48]{0:T(128)}, u32[]{:S(2)}) copy-start(s32[48]{0:T(128)} %param.15) | copy-start | bytes 580
  85.6 10.2 %copy-start.4 = (bf16[48,4,2048]{2,1,0:T(4,128)(2,1)S(1)}, bf16[48,4,2048]{2,1,0:T(4,128)(2,1)}, u32[]{:S(2)}) copy-start(bf16[48,4,2048]{2,1,0:T(4,128)(2,1)} %copy-done.3) | copy-start | bytes 2359300
  126.3 2.2 %copy-start.6 = (bf16[1,192,256]{2,1,0:T(8,128)(2,1)S(1)}, bf16[1,192,256]{2,1,0:T(8,128)(2,1)}, u32[]{:S(2)}) copy-start(bf16[1,192,256]{2,1,0:T(8,128)(2,1)} %get-tuple-element.28) | copy-start | bytes 294916
  128.5 1.8 %copy-start = (bf16[48,4,2,8,28]{4,3,1,2,0:T(8,128)(2,1)S(1)}, bf16[48,4,2,8,28]{4,3,1,2,0:T(8,128)(2,1)}, u32[]{:S(2)}) copy-start(bf16[48,4,2,8,28]{4,3,1,2,0:T(8,128)(2,1)} %divide_convert_fusion) | copy-start | bytes 516100
Sparse Core Ops, SparseCore 0:
  10.2 12.4 reduce-scatter.1
  30.2 55.5 all-gather.1
